TPU v7x, 512 devices: a whole 4x4x16 slice. The times are simulated.
512 devices in a mesh: dp: 8 (over y, x_hi), row: 16 (over z), col: 4 (over x_lo, core).
Axes of the slice: x: 4 (x_hi: 2, x_lo: 2; x = x_hi * 2 + x_lo), y: 4, z: 16, core: 2. Of those that a mesh axis runs over, the one named last changes fastest.
Arguments:
- gate_pre: bfloat16 [4096, 14336], P(('dp', 'col'), 'row'), may hold values from -6 to 6
- up_pre: bfloat16 [4096, 14336], P(('dp', 'col'), 'row'), may hold values from -6 to 6
- out_grad: bfloat16 [4096, 4096], P(('dp', 'row'), 'col'), may hold values from -6 to 6
- down_weight: bfloat16 [14336, 4096], P('row', 'col'), may hold values from -0.046875 to 0.046875
Outputs:
- layer_out: bfloat16 [4096, 4096], P(('dp', 'row'), 'col')
- gate_grad: bfloat16 [4096, 14336], P(('dp', 'col'), 'row')
- up_grad: bfloat16 [4096, 14336], P(('dp', 'col'), 'row')
- weight_grad: float32 [14336, 4096], P(('row', 'dp'), 'col')
All inputs are finite; a program needn't handle non-finite values.
Results may differ from a plain program's by a relative error of at most 0.017.
Values may be sent and summed in bfloat16 or wider, within the bound.
No kernel may reach another device: no remote copies, remote signals or barrier semaphores. Data moves between devices by JAX's collectives and lax.ppermute only.
A program may use at most 64 MiB of HBM per device.

v0:
```python
import jax
import jax.numpy as jnp
from jax import lax
from jax.sharding import PartitionSpec as P


def shards(gate_pre, up_pre, out_grad, down_weight):
    gate32 = gate_pre.astype(jnp.float32)
    up32 = up_pre.astype(jnp.float32)
    sgate = jax.nn.sigmoid(gate32)
    act = gate32 * sgate
    hidden = (act * up32).astype(jnp.bfloat16)
    hidden_all = lax.all_gather(hidden, "col", axis=0, tiled=True)
    rows = hidden_all
    layer_out = lax.psum_scatter(
        jnp.dot(rows, down_weight, preferred_element_type=jnp.float32).astype(jnp.bfloat16),
        "row",
        scatter_dimension=0,
        tiled=True,
    )
    grad_all = lax.all_gather(out_grad, "row", axis=0, tiled=True)
    rows = grad_all
    dhidden = lax.psum_scatter(
        lax.dot_general(
            rows, down_weight, (((1,), (1,)), ((), ())), preferred_element_type=jnp.float32
        ).astype(jnp.bfloat16),
        "col",
        scatter_dimension=0,
        tiled=True,
    ).astype(jnp.float32)
    up_grad = (dhidden * act).astype(jnp.bfloat16)
    gate_grad = (dhidden * up32 * sgate * (1.0 + gate32 * (1.0 - sgate))).astype(jnp.bfloat16)
    replica_count = lax.axis_size("dp")
    factor = 1.0 / (hidden_all.shape[0] * replica_count) ** 0.5
    local_grad = (
        lax.dot_general(
            hidden_all, grad_all, (((0,), (0,)), ((), ())), preferred_element_type=jnp.float32
        )
        * factor
    )
    weight_grad = lax.psum_scatter(
        local_grad.astype(jnp.bfloat16), "dp", scatter_dimension=0, tiled=True
    ).astype(jnp.float32)
    return (layer_out, gate_grad, up_grad, weight_grad)


def solution(mesh):
    return jax.shard_map(
        shards,
        mesh=mesh,
        in_specs=(
            P(("dp", "col"), "row"),
            P(("dp", "col"), "row"),
            P(("dp", "row"), "col"),
            P("row", "col"),
        ),
        out_specs=(
            P(("dp", "row"), "col"),
            P(("dp", "col"), "row"),
            P(("dp", "col"), "row"),
            P(("row", "dp"), "col"),
        ),
        check_vma=False,
    )
```

profile of v0, /device:TPU:2, one launch (start us, length us, event | category | flops | bytes accessed | tf_op | source)
XLA Modules:
  0.0 299.6 jit_solution(961609800067934106)
XLA Ops:
  7.2 0.0 copy-start
  7.2 0.0 all-gather.2.cloned.1.call-start
  7.2 0.7 all-gather.2.cloned.1.call-update
  7.9 0.0 copy-start.1
  7.9 0.0 copy-start.2
  7.9 0.0 reduce-scatter.6.cloned.1.call-start
  8.0 77.3 %all-gather.2.cloned.1.call-done = bf16[512,1024]{1,0:T(8,128)(2,1)} async-done(((bf16[32,1024]{1,0:T(8,128)(2,1)}), bf16[512,1024]{1,0:T(8,128)(2,1)}) %all-gather.2.cloned.1.call-update) | async-done | bytes 1048592 | tf_op jit(solution)/shard_map/all_gather | solution.py:21
  85.2 0.0 copy-done
  85.2 3.5 %convolution_convert_fusion.1 = bf16[512,896]{1,0:T(8,128)(2,1)} fusion(bf16[512,1024]{1,0:T(8,128)(2,1)} %all-gather.2.cloned.1.call-done, bf16[896,1024]{1,0:T(8,128)(2,1)S(1)} %copy-done), kind=kOutput, calls=%fused_computation.2 | convolution fusion | flops 939982848 | bytes 3801088 | tf_op jit(solution)/shard_map/dot_general | solution.py:24
  88.7 0.0 reduce-scatter.6.cloned.1.call-update
  88.7 0.0 reduce-scatter.8.cloned.1.call-start
  88.8 23.1 %reduce-scatter.6.cloned.1.call-done = bf16[128,896]{1,0:T(8,128)(2,1)} async-done(((bf16[512,896]{1,0:T(8,128)(2,1)}), bf16[128,896]{1,0:T(8,128)(2,1)}) %reduce-scatter.6.cloned.1.call-update) | async-done | bytes 229392 | tf_op jit(solution)/shard_map/reduce_scatter | solution.py:23
  111.8 0.0 copy-done.1
  111.8 0.0 copy-done.2
  111.8 2.0 fusion.4
  113.8 9.8 %all_gather.6 = bf16[512,896]{1,0:T(8,128)(2,1)S(1)} all-gather(bf16[128,896]{1,0:T(8,128)(2,1)S(1)} %get-tuple-element.6), channel_id=1, replica_groups=mesh['dp'=8,'row'=16,'col'=4] {'col'}, dimensions={0}, use_global_device_ids=true | all-gather | bytes 1146880 | tf_op jit(solution)/shard_map/all_gather | solution.py:13
  123.6 3.6 %multiply_convert_fusion = bf16[896,1024]{1,0:T(8,128)(2,1)} fusion(bf16[512,896]{1,0:T(8,128)(2,1)S(1)} %all_gather.6, bf16[512,1024]{1,0:T(8,128)(2,1)} %all-gather.2.cloned.1.call-done), kind=kOutput, calls=%fused_computation | convolution fusion | flops 941359104 | bytes 3801088 | tf_op jit(solution)/shard_map/dot_general | solution.py:36
  127.3 0.0 reduce-scatter.8.cloned.1.call-update
  127.3 0.0 reduce-scatter.4.cloned.1.call-start
  127.3 2.2 convolution_convert_fusion
  129.5 0.0 reduce-scatter.4.cloned.1.call-update
  129.6 89.1 %reduce-scatter.8.cloned.1.call-done = bf16[112,1024]{1,0:T(8,128)(2,1)} async-done(((bf16[896,1024]{1,0:T(8,128)(2,1)}), bf16[112,1024]{1,0:T(8,128)(2,1)}) %reduce-scatter.8.cloned.1.call-update) | async-done | bytes 229392 | tf_op jit(solution)/shard_map/reduce_scatter | solution.py:41
  218.6 1.7 convert_element_type.39
  220.4 72.7 %reduce-scatter.4.cloned.1.call-done = bf16[32,1024]{1,0:T(8,128)(2,1)} async-done(((bf16[512,1024]{1,0:T(8,128)(2,1)}), bf16[32,1024]{1,0:T(8,128)(2,1)}) %reduce-scatter.4.cloned.1.call-update) | async-done | bytes 65552 | tf_op jit(solution)/shard_map/reduce_scatter | solution.py:15
Async XLA Ops:
  7.2 78.1 %copy-start = (bf16[896,1024]{1,0:T(8,128)(2,1)S(1)}, bf16[896,1024]{1,0:T(8,128)(2,1)}, u32[]{:S(2)}) copy-start(bf16[896,1024]{1,0:T(8,128)(2,1)} %param.7) | copy-start | bytes 5505028
  7.2 78.1 %all-gather.2.cloned.1.call-start = ((), (), s32[]{:S(2)}) async-start(), calls=%async_computation.4 | async-start | bytes 1114112 | tf_op jit(solution)/shard_map/all_gather | solution.py:21
  7.9 103.9 %copy-start.1 = (bf16[128,896]{1,0:T(8,128)(2,1)S(1)}, bf16[128,896]{1,0:T(8,128)(2,1)}, u32[]{:S(2)}) copy-start(bf16[128,896]{1,0:T(8,128)(2,1)} %param.4) | copy-start | bytes 688132
  7.9 103.9 %copy-start.2 = (bf16[128,896]{1,0:T(8,128)(2,1)S(1)}, bf16[128,896]{1,0:T(8,128)(2,1)}, u32[]{:S(2)}) copy-start(bf16[128,896]{1,0:T(8,128)(2,1)} %param.5) | copy-start | bytes 688132
  7.9 103.9 %reduce-scatter.6.cloned.1.call-start = ((), (), s32[]{:S(2)}) async-start(), calls=%async_computation.5 | async-start | bytes 1146880 | tf_op jit(solution)/shard_map/reduce_scatter | solution.py:23
  88.7 129.9 %reduce-scatter.8.cloned.1.call-start = ((), (), s32[]{:S(2)}) async-start(), calls=%async_computation.6 | async-start | bytes 2064384 | tf_op jit(solution)/shard_map/reduce_scatter | solution.py:41
  127.3 165.8 %reduce-scatter.4.cloned.1.call-start = ((), (), s32[]{:S(2)}) async-start(), calls=%async_computation.3 | async-start | bytes 1114112 | tf_op jit(solution)/shard_map/reduce_scatter | solution.py:15
Sparse Core Ops, SparseCore 0:
  10.1 75.1 all-gather.1
  88.8 22.9 reduce-scatter.5
  127.4 91.1 reduce-scatter.7
  221.9 71.1 reduce-scatter.3
where the time goes:
time: 300 us
  waiting for transfers between devices  263 us (88%)
  between operations  13.8 us (5%)
  blocking collectives  9.81 us (3%)
  matrix products  9.29 us (3%)
  other arithmetic  3.73 us (1%)
    reduce_scatter x1, waiting for transfers between devices, shards(): lax.psum_scatter(local_grad.astype(jnp.bfloat16), 'dp', scatter_dimension...  89.1 us
    all_gather x1, waiting for transfers between devices, shards(): grad_all = lax.all_gather(out_grad, 'row', axis=0, tiled=True)  77.3 us
    reduce_scatter x1, waiting for transfers between devices, shards(): lax.psum_scatter(jnp.dot(rows, down_weight, preferred_element_type=jnp.fl...  72.7 us
    reduce_scatter x1, waiting for transfers between devices, shards(): lax.psum_scatter(lax.dot_general(rows, down_weight, (((1,), (1,)), ((), (...  23.1 us
    all_gather x1, blocking collectives, shards(): hidden_all = lax.all_gather(hidden, 'col', axis=0, tiled=True)  9.81 us
  transfers between devices with their start and end apart: 4, of which 4 were waited for; matrix products, arithmetic and copies ran while one was open for 1% of the time, Pallas kernels for 0%

commit v1 on v0

v1 whole, which is shorter than its diff:
```python
import jax
import jax.numpy as jnp
from jax import lax
from jax.sharding import PartitionSpec as P

hold = lax.optimization_barrier


def exchange_sum(parts, axis):
    count = lax.axis_size(axis)
    parts = parts.reshape((count, parts.shape[0] // count) + parts.shape[1:])
    parts = lax.all_to_all(parts, axis, 0, 0, tiled=True)
    return jnp.sum(parts.astype(jnp.float32), axis=0)


def shards(gate_pre, up_pre, out_grad, down_weight):
    gate32 = gate_pre.astype(jnp.float32)
    up32 = up_pre.astype(jnp.float32)
    sgate = jax.nn.sigmoid(gate32)
    act = gate32 * sgate
    hidden = hold((act * up32).astype(jnp.bfloat16))
    hidden_all = lax.all_gather(hidden, "col", axis=0, tiled=True)
    layer_parts = jnp.dot(hidden_all, down_weight, preferred_element_type=jnp.float32).astype(jnp.bfloat16)
    layer_out = exchange_sum(layer_parts, "row").astype(jnp.bfloat16)

    half = out_grad.shape[1] // 2
    grad_all = jnp.concatenate(
        [
            lax.all_gather(out_grad[:, :half], "row", axis=0, tiled=True),
            lax.all_gather(out_grad[:, half:], "row", axis=0, tiled=True),
        ],
        axis=1,
    )
    hidden_all, grad_all = hold((hidden_all, grad_all))
    dhidden = exchange_sum(
        lax.dot_general(
            grad_all, down_weight, (((1,), (1,)), ((), ())), preferred_element_type=jnp.float32
        ).astype(jnp.bfloat16),
        "col",
    )
    up_grad = (dhidden * act).astype(jnp.bfloat16)
    gate_grad = (dhidden * up32 * sgate * (1.0 + gate32 * (1.0 - sgate))).astype(jnp.bfloat16)
    factor = 1.0 / (hidden_all.shape[0] * lax.axis_size("dp")) ** 0.5
    local_grad = (
        lax.dot_general(
            hidden_all, grad_all, (((0,), (0,)), ((), ())), preferred_element_type=jnp.float32
        )
        * factor
    )
    weight_grad = exchange_sum(local_grad.astype(jnp.bfloat16), "dp")
    return (layer_out, gate_grad, up_grad, weight_grad)


def solution(mesh):
    return jax.shard_map(
        shards,
        mesh=mesh,
        in_specs=(
            P(("dp", "col"), "row"),
            P(("dp", "col"), "row"),
            P(("dp", "row"), "col"),
            P("row", "col"),
        ),
        out_specs=(
            P(("dp", "row"), "col"),
            P(("dp", "col"), "row"),
            P(("dp", "col"), "row"),
            P(("row", "dp"), "col"),
        ),
        check_vma=False,
    )
```

time: 300 us -> 188 us (0.63)
  the two profiles are of different devices: /device:TPU:2 before, /device:TPU:32 now
where the time goes in v1:
time: 188 us; the launch traced here: 187 us
  blocking collectives  76.9 us (41%)
  waiting for transfers between devices  73.7 us (39%)
  starting transfers between devices  18 us (10%)
  matrix products  9.55 us (5%)
  other arithmetic  7.26 us (4%)
    all_to_all x3, waiting for transfers between devices, exchange_sum(): parts = lax.all_to_all(parts, axis, 0, 0, tiled=True)  73.7 us
    all_gather x1, blocking collectives, shards(): lax.all_gather(out_grad[:, half:], 'row', axis=0, tiled=True)  36.4 us
    all_gather x1, blocking collectives, shards(): lax.all_gather(out_grad[:, :half], 'row', axis=0, tiled=True)  30.8 us
    all_to_all x3, starting transfers between devices, exchange_sum(): parts = lax.all_to_all(parts, axis, 0, 0, tiled=True)  18 us
    all_gather x1, blocking collectives, shards(): hidden_all = lax.all_gather(hidden, 'col', axis=0, tiled=True)  9.76 us
    reduce_sum x3, other arithmetic, exchange_sum(): return jnp.sum(parts.astype(jnp.float32), axis=0)  4.8 us
    dot_general x1, matrix products, shards(): lax.dot_general(hidden_all, grad_all, (((0,), (0,)), ((), ())), preferred...  3.9 us
  transfers between devices with their start and end apart: 3, of which 3 were waited for; matrix products, arithmetic and copies ran while one was open for 7% of the time, Pallas kernels for 0%

profile of v1, /device:TPU:32, one launch (start us, length us, event | category | flops | bytes accessed | tf_op | source)
XLA Modules:
  0.0 187.1 jit_solution(10193498037429948498)
XLA Ops:
  0.6 0.0 copy-start
  0.6 0.0 copy-start.5
  0.7 1.4 fusion
  2.0 9.8 %all_gather.9 = bf16[512,896]{1,0:T(8,128)(2,1)} all-gather(bf16[128,896]{1,0:T(8,128)(2,1)S(1)} %fusion), channel_id=1, replica_groups=mesh['dp'=8,'row'=16,'col'=4] {'col'}, dimensions={0}, use_global_device_ids=true | all-gather | bytes 1146880 | tf_op jit(solution)/shard_map/all_gather | solution.py:22
  11.8 0.0 copy-done.5
  11.8 36.4 %all_gather.11 = bf16[512,512]{1,0:T(8,128)(2,1)S(1)} all-gather(bf16[32,512]{1,0:T(8,128)(2,1)S(1)} %get-tuple-element.11), channel_id=1, replica_groups=mesh['dp'=8,'row'=16,'col'=4] {'row'}, dimensions={0}, use_global_device_ids=true | all-gather | bytes 557056 | tf_op jit(solution)/shard_map/all_gather | solution.py:30
  48.2 30.8 %all_gather.10 = bf16[512,512]{1,0:T(8,128)(2,1)S(1)} all-gather(bf16[32,512]{1,0:T(8,128)(2,1)S(1)} %get-tuple-element.10), channel_id=1, replica_groups=mesh['dp'=8,'row'=16,'col'=4] {'row'}, dimensions={0}, use_global_device_ids=true | all-gather | bytes 557056 | tf_op jit(solution)/shard_map/all_gather | solution.py:29
  78.9 0.1 pad_maximum_fusion
  79.1 0.0 copy-done
  79.1 2.2 %convolution_convert_fusion.1 = bf16[512,896]{1,0:T(8,128)(2,1)} fusion(bf16[512,1024]{1,0:T(8,128)(2,1)S(1)} %pad_maximum_fusion, bf16[896,1024]{1,0:T(8,128)(2,1)S(1)} %copy-done), kind=kOutput, calls=%fused_computation.4 | convolution fusion | flops 939982848 | bytes 3801088 | tf_op jit(solution)/shard_map/dot_general | solution.py:36
  81.3 0.0 copy-done.2
  81.3 3.5 %all-to-all-start.1 = ((bf16[4,128,896]{2,1,0:T(8,128)(2,1)}), bf16[4,128,896]{2,1,0:T(8,128)(2,1)S(1)}, u32[]{:S(2)}, u32[]{:S(2)}) async-start(bf16[4,128,896]{2,1,0:T(8,128)(2,1)} %bitcast.11), calls=%async_computation.1 | async-start | bytes 1835008 | tf_op jit(solution)/shard_map/all_to_all | solution.py:12
  84.8 3.9 %multiply_convert_fusion = bf16[896,1024]{1,0:T(8,128)(2,1)} fusion(bf16[512,896]{1,0:T(8,128)(2,1)} %all_gather.9, bf16[512,1024]{1,0:T(8,128)(2,1)} %copy-done.2), kind=kOutput, calls=%fused_computation.1 | convolution fusion | flops 941359104 | bytes 3801088 | tf_op jit(solution)/shard_map/dot_general | solution.py:45
  88.7 9.1 %all-to-all-done.1 = bf16[4,128,896]{2,1,0:T(8,128)(2,1)S(1)} async-done(((bf16[4,128,896]{2,1,0:T(8,128)(2,1)}), bf16[4,128,896]{2,1,0:T(8,128)(2,1)S(1)}, u32[]{:S(2)}, u32[]{:S(2)}) %all-to-all-start.1) | async-done | bytes 917536 | tf_op jit(solution)/shard_map/all_to_all | solution.py:12
  97.8 0.9 copy-done.1
  98.8 6.6 %all-to-all-start.2 = ((bf16[8,112,1024]{2,1,0:T(8,128)(2,1)}), bf16[8,112,1024]{2,1,0:T(8,128)(2,1)}, u32[]{:S(2)}, u32[]{:S(2)}) async-start(bf16[8,112,1024]{2,1,0:T(8,128)(2,1)} %bitcast.9), calls=%async_computation.2 | async-start | bytes 3670016 | tf_op jit(solution)/shard_map/all_to_all | solution.py:12
  105.4 3.4 %convolution_convert_fusion = bf16[512,1024]{1,0:T(8,128)(2,1)} fusion(bf16[512,896]{1,0:T(8,128)(2,1)} %all_gather.9, bf16[896,1024]{1,0:T(8,128)(2,1)S(1)} %copy-done), kind=kOutput, calls=%fused_computation.3 | convolution fusion | flops 940048384 | bytes 3801088 | tf_op jit(solution)/shard_map/dot_general | solution.py:23
  108.8 22.1 %all-to-all-done.2 = bf16[8,112,1024]{2,1,0:T(8,128)(2,1)} async-done(((bf16[8,112,1024]{2,1,0:T(8,128)(2,1)}), bf16[8,112,1024]{2,1,0:T(8,128)(2,1)}, u32[]{:S(2)}, u32[]{:S(2)}) %all-to-all-start.2) | async-done | bytes 1835040 | tf_op jit(solution)/shard_map/all_to_all | solution.py:12
  130.9 7.8 %all-to-all-start = ((bf16[16,32,1024]{2,1,0:T(8,128)(2,1)}), bf16[16,32,1024]{2,1,0:T(8,128)(2,1)S(1)}, u32[]{:S(2)}, u32[]{:S(2)}) async-start(bf16[16,32,1024]{2,1,0:T(8,128)(2,1)} %bitcast.10), calls=%async_computation | async-start | bytes 2097152 | tf_op jit(solution)/shard_map/all_to_all | solution.py:12
  138.7 1.4 convert_reduce_fusion.1
  140.1 1.0 multiply_convert_fusion.1
  141.1 2.6 %convert_reduce_fusion = f32[112,1024]{1,0:T(8,128)} fusion(bf16[8,112,1024]{2,1,0:T(8,128)(2,1)} %all-to-all-done.2), kind=kLoop, calls=%fused_computation | loop fusion | flops 1720320 | bytes 2293760 | tf_op jit(solution)/shard_map/reduce_sum | solution.py:13
  143.7 42.6 %all-to-all-done = bf16[16,32,1024]{2,1,0:T(8,128)(2,1)S(1)} async-done(((bf16[16,32,1024]{2,1,0:T(8,128)(2,1)}), bf16[16,32,1024]{2,1,0:T(8,128)(2,1)S(1)}, u32[]{:S(2)}, u32[]{:S(2)}) %all-to-all-start) | async-done | bytes 1048608 | tf_op jit(solution)/shard_map/all_to_all | solution.py:12
  186.3 0.8 reduce_sum.30
  (7 shorter events, 0.0 us)
Async XLA Ops:
  0.6 78.4 %copy-start = (bf16[896,1024]{1,0:T(8,128)(2,1)S(1)}, bf16[896,1024]{1,0:T(8,128)(2,1)}, u32[]{:S(2)}) copy-start(bf16[896,1024]{1,0:T(8,128)(2,1)} %param.7) | copy-start | bytes 5505028
  0.6 11.1 %copy-start.5 = (bf16[32,1024]{1,0:T(8,128)(2,1)S(1)}, bf16[32,1024]{1,0:T(8,128)(2,1)}, u32[]{:S(2)}) copy-start(bf16[32,1024]{1,0:T(8,128)(2,1)} %param.6) | copy-start | bytes 196612
  79.1 2.2 %copy-start.2 = (bf16[512,1024]{1,0:T(8,128)(2,1)}, bf16[512,1024]{1,0:T(8,128)(2,1)S(1)}, u32[]{:S(2)}) copy-start(bf16[512,1024]{1,0:T(8,128)(2,1)S(1)} %pad_maximum_fusion) | copy-start | bytes 3145732
  81.3 16.5 %all-to-all-start.1 = ((bf16[4,128,896]{2,1,0:T(8,128)(2,1)}), bf16[4,128,896]{2,1,0:T(8,128)(2,1)S(1)}, u32[]{:S(2)}, u32[]{:S(2)}) async-start(bf16[4,128,896]{2,1,0:T(8,128)(2,1)} %bitcast.11), calls=%async_computation.1 | async-start | bytes 1835008 | tf_op jit(solution)/shard_map/all_to_all | solution.py:12
  97.8 0.9 copy-start.1
  98.8 32.1 %all-to-all-start.2 = ((bf16[8,112,1024]{2,1,0:T(8,128)(2,1)}), bf16[8,112,1024]{2,1,0:T(8,128)(2,1)}, u32[]{:S(2)}, u32[]{:S(2)}) async-start(bf16[8,112,1024]{2,1,0:T(8,128)(2,1)} %bitcast.9), calls=%async_computation.2 | async-start | bytes 3670016 | tf_op jit(solution)/shard_map/all_to_all | solution.py:12
  108.8 31.2 %copy-start.3 = (bf16[128,896]{1,0:T(8,128)(2,1)S(1)}, bf16[128,896]{1,0:T(8,128)(2,1)}, u32[]{:S(2)}) copy-start(bf16[128,896]{1,0:T(8,128)(2,1)} %param.5) | copy-start | bytes 688132
  108.8 31.2 %copy-start.4 = (bf16[128,896]{1,0:T(8,128)(2,1)S(1)}, bf16[128,896]{1,0:T(8,128)(2,1)}, u32[]{:S(2)}) copy-start(bf16[128,896]{1,0:T(8,128)(2,1)} %param.4) | copy-start | bytes 688132
  130.9 55.4 %all-to-all-start = ((bf16[16,32,1024]{2,1,0:T(8,128)(2,1)}), bf16[16,32,1024]{2,1,0:T(8,128)(2,1)S(1)}, u32[]{:S(2)}, u32[]{:S(2)}) async-start(bf16[16,32,1024]{2,1,0:T(8,128)(2,1)} %bitcast.10), calls=%async_computation | async-start | bytes 2097152 | tf_op jit(solution)/shard_map/all_to_all | solution.py:12
